TPU v7x, 32 devices: a whole 2x2x4 slice. The times are simulated.
32 devices in a mesh: cand: 4 (over y, core), hid: 8 (over z, x).
Axes of the slice: x: 2, y: 2, z: 4, core: 2. Of those that a mesh axis runs over, the one named last changes fastest.
Arguments:
- tokens: bfloat16 [4, 256, 2048], P('cand', None, 'hid'), may hold values from -6 to 6
- cotangent: bfloat16 [4, 256, 2048], P('cand', None, 'hid'), may hold values from -6 to 6
- gate_weight: bfloat16 [2048, 8192], P('cand', 'hid'), may hold values from -0.125 to 0.125
- up_weight: bfloat16 [2048, 8192], P('cand', 'hid'), may hold values from -0.125 to 0.125
- down_weight: bfloat16 [8192, 2048], P('hid', 'cand'), may hold values from -0.125 to 0.125
- width_steps: int32 [4], P('cand'), may hold values from 1 to 8
- block_order: int32 [8], replicated, may hold values from 0 to 7, each once
Outputs:
- grad_tokens: float32 [4, 256, 2048], P('cand', None, 'hid')
- grad_gate: float32 [2048, 8192], P('cand', 'hid')
- grad_up: float32 [2048, 8192], P('cand', 'hid')
- grad_down: float32 [8192, 2048], P('hid', 'cand')
Inputs may be any that keep to these rules, and one draw needn't show every extreme that they name: Candidate c uses the first width_steps[c] * 1024 logical hidden units. `block_order`: names each of the 8 logical blocks once.
All inputs are finite; a program needn't handle non-finite values.
Results may differ from a plain program's by a relative error of at most 0.02.
Values may be sent and summed in bfloat16 or wider, within the bound.
A program may use at most 64 MiB of HBM per device.

v0:
```python
import jax
import jax.numpy as jnp
from jax import lax
from jax.sharding import PartitionSpec as P

FF = 8192


def shards(tokens, cotangent, gate_weight, up_weight, down_weight, width_steps, block_order):
    inputs, upstream = (
        lax.all_gather(tokens, "hid", axis=2, tiled=True),
        lax.all_gather(cotangent, "hid", axis=2, tiled=True),
    )
    inputs = inputs[0]
    upstream = upstream[0]
    gate_full, up_full = (
        lax.all_gather(gate_weight, "cand", axis=0, tiled=True),
        lax.all_gather(up_weight, "cand", axis=0, tiled=True),
    )
    down_full = lax.all_gather(down_weight, "cand", axis=1, tiled=True)
    width = gate_weight.shape[1]
    places = jnp.arange(block_order.shape[0], dtype=jnp.int32)
    logical = jnp.sum(jnp.where(places == lax.axis_index("hid"), block_order, 0))
    active = logical * width < width_steps[0] * (FF // 8)
    keep = active.astype(jnp.float32)
    gate = jnp.dot(inputs, gate_full, preferred_element_type=jnp.float32)
    up = jnp.dot(inputs, up_full, preferred_element_type=jnp.float32)
    sig = jax.nn.sigmoid(gate)
    act = keep * gate * sig
    hidden = (act * up).astype(jnp.bfloat16)
    dhid = keep * jnp.einsum("td,fd->tf", upstream, down_full, preferred_element_type=jnp.float32)
    forward_d_up = (dhid * act).astype(jnp.bfloat16)
    forward_d_gate = (dhid * up * keep * sig * (1.0 + gate * (1.0 - sig))).astype(jnp.bfloat16)
    down_local = jnp.einsum("tf,td->fd", hidden, upstream, preferred_element_type=jnp.float32)
    down_local, d_gate, d_up = (down_local, forward_d_gate, forward_d_up)
    gate_local = jnp.einsum("td,tf->df", inputs, d_gate, preferred_element_type=jnp.float32)
    up_local = jnp.einsum("td,tf->df", inputs, d_up, preferred_element_type=jnp.float32)
    input_part = jnp.einsum("tf,df->td", d_gate, gate_full, preferred_element_type=jnp.float32)
    input_part = input_part + jnp.einsum(
        "tf,df->td", d_up, up_full, preferred_element_type=jnp.float32
    )
    gate_local, up_local, input_part = (gate_local, up_local, input_part)
    grad_tokens = lax.psum_scatter(
        input_part[None].astype(jnp.bfloat16), "hid", scatter_dimension=2, tiled=True
    ).astype(jnp.float32)
    grad_gate, grad_up = (
        lax.psum_scatter(
            gate_local.astype(jnp.bfloat16), "cand", scatter_dimension=0, tiled=True
        ).astype(jnp.float32),
        lax.psum_scatter(
            up_local.astype(jnp.bfloat16), "cand", scatter_dimension=0, tiled=True
        ).astype(jnp.float32),
    )
    grad_down = lax.psum_scatter(
        down_local.astype(jnp.bfloat16), "cand", scatter_dimension=1, tiled=True
    ).astype(jnp.float32)
    return (grad_tokens, grad_gate, grad_up, grad_down)


def solution(mesh):
    in_specs = (
        P("cand", None, "hid"),
        P("cand", None, "hid"),
        P("cand", "hid"),
        P("cand", "hid"),
        P("hid", "cand"),
        P("cand"),
        P(),
    )
    out_specs = (P("cand", None, "hid"), P("cand", "hid"), P("cand", "hid"), P("hid", "cand"))
    return jax.shard_map(shards, mesh=mesh, in_specs=in_specs, out_specs=out_specs, check_vma=False)
```

profile of v0, /device:TPU:0, one launch (start us, length us, event | category | flops | bytes accessed | tf_op | source)
XLA Modules:
  0.0 422.3 jit_solution(7583610765798703201)
XLA Ops:
  7.2 0.0 all-gather.10.cloned.1.call-start
  7.2 0.7 all-gather.10.cloned.1.call-update
  7.9 0.0 all-gather.12.cloned.1.call-start
  7.9 0.7 all-gather.12.cloned.1.call-update
  8.6 0.0 all-gather.14.cloned.1.call-start
  8.7 0.7 all-gather.14.cloned.1.call-update
  9.4 0.0 all-gather.6.cloned.1.call-start
  9.4 0.5 all-gather.6.cloned.1.call-update
  10.0 0.0 all-gather.8.cloned.1.call-start
  10.0 0.5 all-gather.8.cloned.1.call-update
  10.5 0.0 reduce-scatter.5.cloned.1.call-start
  11.2 1.3 fusion.10
  13.2 39.0 %all-gather.10.cloned.1.call-done = bf16[1,256,2048]{2,1,0:T(8,128)(2,1)} async-done(((bf16[1,256,256]{2,1,0:T(8,128)(2,1)}), bf16[1,256,2048]{2,1,0:T(8,128)(2,1)}) %all-gather.10.cloned.1.call-update) | async-done | bytes 1048592 | tf_op jit(solution)/shard_map/all_gather | solution.py:11
  52.2 0.0 copy-start
  52.2 35.1 %all-gather.12.cloned.1.call-done = bf16[2048,1024]{1,0:T(8,128)(2,1)} async-done(((bf16[512,1024]{1,0:T(8,128)(2,1)}), bf16[2048,1024]{1,0:T(8,128)(2,1)}) %all-gather.12.cloned.1.call-update) | async-done | bytes 4194320 | tf_op jit(solution)/shard_map/all_gather | solution.py:18
  87.2 3.8 fusion.6
  91.0 0.0 copy-start.4
  91.0 32.3 %all-gather.14.cloned.1.call-done = bf16[2048,1024]{1,0:T(8,128)(2,1)} async-done(((bf16[512,1024]{1,0:T(8,128)(2,1)}), bf16[2048,1024]{1,0:T(8,128)(2,1)}) %all-gather.14.cloned.1.call-update) | async-done | bytes 4194320 | tf_op jit(solution)/shard_map/all_gather | solution.py:17
  123.3 0.0 copy-done
  123.3 4.4 %fusion.4 = f32[256,1024]{1,0:T(8,128)} fusion(bf16[2048,1024]{1,0:T(8,128)(2,1)} %all-gather.14.cloned.1.call-done, bf16[1,256,2048]{2,1,0:T(8,128)(2,1)S(1)} %copy-done), kind=kOutput, calls=%fused_computation.9 | convolution fusion | flops 1073741824 | bytes 6291456 | tf_op jit(solution)/shard_map/dot_general | solution.py:26
  127.7 36.9 %all-gather.6.cloned.1.call-done = bf16[1,256,2048]{2,1,0:T(8,128)(2,1)} async-done(((bf16[1,256,256]{2,1,0:T(8,128)(2,1)}), bf16[1,256,2048]{2,1,0:T(8,128)(2,1)}) %all-gather.6.cloned.1.call-update) | async-done | bytes 1048592 | tf_op jit(solution)/shard_map/all_gather | solution.py:12
  164.6 34.9 %all-gather.8.cloned.1.call-done = bf16[1024,2048]{1,0:T(8,128)(2,1)} async-done(((bf16[1024,512]{1,0:T(8,128)(2,1)}), bf16[1024,2048]{1,0:T(8,128)(2,1)}) %all-gather.8.cloned.1.call-update) | async-done | bytes 4194320 | tf_op jit(solution)/shard_map/all_gather | solution.py:20
  199.5 4.6 %multiply_convert_fusion.1 = (bf16[256,1024]{1,0:T(8,128)(2,1)S(1)}, bf16[256,1024]{1,0:T(8,128)(2,1)S(1)}) fusion(f32[256,1024]{1,0:T(8,128)} %fusion.4, f32[]{:T(128)S(6)} %convert_element_type.45, f32[256,1024]{1,0:T(8,128)S(1)} %fusion.6, bf16[1024,2048]{1,0:T(8,128)(2,1)} %all-gather.8.cloned.1.call-done, ...), kind=kOutput, calls=%fused_computation.16 | convolution fusion | flops 1077936128 | bytes 8388612 | tf_op jit(solution)/shard_map/td,fd->tf/dot_general | solution.py:31
  204.1 0.0 copy-done.4
  204.1 0.0 copy-start.1
  204.1 0.0 copy-done.2
  204.2 1.3 fusion.12
  205.4 0.9 copy-done.1
  206.3 2.3 fusion.1
  208.6 0.0 reduce-scatter.5.cloned.1.call-update
  208.6 0.0 reduce-scatter.11.cloned.1.call-start
  208.7 0.0 copy-done.3
  208.7 4.9 %convolution_convert_fusion = bf16[1024,2048]{1,0:T(8,128)(2,1)} fusion(bf16[1,256,2048]{2,1,0:T(8,128)(2,1)S(1)} %copy-done.3, f32[256,1024]{1,0:T(8,128)} %copy-done.4, f32[256,1024]{1,0:T(8,128)} %fusion.4, f32[]{:T(128)S(6)} %convert_element_type.45), kind=kOutput, calls=%fused_computation.2 | convolution fusion | flops 1077673984 | bytes 7340036 | tf_op jit(solution)/shard_map/tf,td->fd/dot_general | solution.py:34
  213.5 0.0 reduce-scatter.11.cloned.1.call-update
  213.6 0.0 reduce-scatter.9.cloned.1.call-start
  213.6 3.3 convert_bitcast_fusion
  216.9 0.0 reduce-scatter.9.cloned.1.call-update
  216.9 0.0 reduce-scatter.7.cloned.1.call-start
  217.0 3.3 convert_bitcast_fusion.1
  220.2 0.0 reduce-scatter.7.cloned.1.call-update
  220.2 53.1 %reduce-scatter.5.cloned.1.call-done = bf16[1,256,256]{2,1,0:T(8,128)(2,1)} async-done(((bf16[1,256,2048]{2,1,0:T(8,128)(2,1)}), bf16[1,256,256]{2,1,0:T(8,128)(2,1)}) %reduce-scatter.5.cloned.1.call-update) | async-done | bytes 131088 | tf_op jit(solution)/shard_map/reduce_scatter | solution.py:43
  273.3 1.6 convert_element_type.50
  275.0 44.3 %reduce-scatter.11.cloned.1.call-done = bf16[1024,512]{1,0:T(8,128)(2,1)} async-done(((bf16[1024,2048]{1,0:T(8,128)(2,1)}), bf16[1024,512]{1,0:T(8,128)(2,1)}) %reduce-scatter.11.cloned.1.call-update) | async-done | bytes 1048592 | tf_op jit(solution)/shard_map/reduce_scatter | solution.py:54
  319.2 2.8 convert_element_type.59
  322.1 44.1 %reduce-scatter.9.cloned.1.call-done = bf16[512,1024]{0,1:T(8,128)(2,1)} async-done(((bf16[2048,1024]{0,1:T(8,128)(2,1)}), bf16[512,1024]{0,1:T(8,128)(2,1)}) %reduce-scatter.9.cloned.1.call-update) | async-done | bytes 1048592 | tf_op jit(solution)/shard_map/reduce_scatter | solution.py:50
  366.2 2.6 copy.12
  368.8 44.4 %reduce-scatter.7.cloned.1.call-done = bf16[512,1024]{0,1:T(8,128)(2,1)} async-done(((bf16[2048,1024]{0,1:T(8,128)(2,1)}), bf16[512,1024]{0,1:T(8,128)(2,1)}) %reduce-scatter.7.cloned.1.call-update) | async-done | bytes 1048592 | tf_op jit(solution)/shard_map/reduce_scatter | solution.py:47
  413.2 2.6 copy.11
  (2 shorter events, 0.0 us)
Async XLA Ops:
  7.2 45.0 %all-gather.10.cloned.1.call-start = ((), (), s32[]{:S(2)}) async-start(), calls=%async_computation.6 | async-start | bytes 1179648 | tf_op jit(solution)/shard_map/all_gather | solution.py:11
  7.9 79.3 %all-gather.12.cloned.1.call-start = ((), (), s32[]{:S(2)}) async-start(), calls=%async_computation.7 | async-start | bytes 5242880 | tf_op jit(solution)/shard_map/all_gather | solution.py:18
  8.6 114.6 %all-gather.14.cloned.1.call-start = ((), (), s32[]{:S(2)}) async-start(), calls=%async_computation.8 | async-start | bytes 5242880 | tf_op jit(solution)/shard_map/all_gather | solution.py:17
  9.4 155.2 %all-gather.6.cloned.1.call-start = ((), (), s32[]{:S(2)}) async-start(), calls=%async_computation.4 | async-start | bytes 1179648 | tf_op jit(solution)/shard_map/all_gather | solution.py:12
  10.0 189.6 %all-gather.8.cloned.1.call-start = ((), (), s32[]{:S(2)}) async-start(), calls=%async_computation.5 | async-start | bytes 5242880 | tf_op jit(solution)/shard_map/all_gather | solution.py:20
  10.5 262.8 %reduce-scatter.5.cloned.1.call-start = ((), (), s32[]{:S(2)}) async-start(), calls=%async_computation.9 | async-start | bytes 1179648 | tf_op jit(solution)/shard_map/reduce_scatter | solution.py:43
  52.2 71.1 %copy-start = (bf16[1,256,2048]{2,1,0:T(8,128)(2,1)S(1)}, bf16[1,256,2048]{2,1,0:T(8,128)(2,1)}, u32[]{:S(2)}) copy-start(bf16[1,256,2048]{2,1,0:T(8,128)(2,1)} %all-gather.10.cloned.1.call-done) | copy-start | bytes 3145732
  91.0 113.1 %copy-start.4 = (f32[256,1024]{1,0:T(8,128)}, f32[256,1024]{1,0:T(8,128)S(1)}, u32[]{:S(2)}) copy-start(f32[256,1024]{1,0:T(8,128)S(1)} %fusion.6) | copy-start | bytes 3145732
  199.5 4.6 %copy-start.2 = (bf16[2048,1024]{1,0:T(8,128)(2,1)S(1)}, bf16[2048,1024]{1,0:T(8,128)(2,1)}, u32[]{:S(2)}) copy-start(bf16[2048,1024]{1,0:T(8,128)(2,1)} %all-gather.14.cloned.1.call-done) | copy-start | bytes 12582916
  204.1 2.2 copy-start.1
  206.3 2.3 copy-start.3
  208.6 110.6 %reduce-scatter.11.cloned.1.call-start = ((), (), s32[]{:S(2)}) async-start(), calls=%async_computation.12 | async-start | bytes 5242880 | tf_op jit(solution)/shard_map/reduce_scatter | solution.py:54
  213.6 152.6 %reduce-scatter.9.cloned.1.call-start = ((), (), s32[]{:S(2)}) async-start(), calls=%async_computation.11 | async-start | bytes 5242880 | tf_op jit(solution)/shard_map/reduce_scatter | solution.py:50
  216.9 196.3 %reduce-scatter.7.cloned.1.call-start = ((), (), s32[]{:S(2)}) async-start(), calls=%async_computation.10 | async-start | bytes 5242880 | tf_op jit(solution)/shard_map/reduce_scatter | solution.py:47
Sparse Core Ops, SparseCore 0:
  10.0 42.1 all-gather.9
  53.7 33.4 all-gather.11
  88.8 34.4 all-gather.13
  125.2 39.3 all-gather.5
  166.0 33.4 all-gather.7
  208.7 64.5 reduce-scatter.4
  275.9 43.3 reduce-scatter.10
  321.8 44.3 reduce-scatter.8
  368.7 44.3 reduce-scatter.6
where the time goes:
time: 423 us; the launch traced here: 422 us
  waiting for transfers between devices  367 us (87%)
  matrix products  27.7 us (7%)
  between operations  15.2 us (4%)
  local copies, waits for them, and re-layouts  6.02 us (1%)
  other arithmetic  5.75 us (1%)
    reduce_scatter x1, waiting for transfers between devices, shards(): lax.psum_scatter(input_part[None].astype(jnp.bfloat16), 'hid', scatter_di...  53.1 us
    reduce_scatter x1, waiting for transfers between devices, shards(): lax.psum_scatter(gate_local.astype(jnp.bfloat16), 'cand', scatter_dimensi...  44.4 us
    reduce_scatter x1, waiting for transfers between devices, shards(): lax.psum_scatter(down_local.astype(jnp.bfloat16), 'cand', scatter_dimensi...  44.3 us
    reduce_scatter x1, waiting for transfers between devices, shards(): lax.psum_scatter(up_local.astype(jnp.bfloat16), 'cand', scatter_dimension...  44.1 us
    all_gather x1, waiting for transfers between devices, shards(): lax.all_gather(tokens, 'hid', axis=2, tiled=True)  39 us
    all_gather x1, waiting for transfers between devices, shards(): lax.all_gather(cotangent, 'hid', axis=2, tiled=True)  36.9 us
    all_gather x1, waiting for transfers between devices, shards(): lax.all_gather(up_weight, 'cand', axis=0, tiled=True)  35.1 us
    all_gather x1, waiting for transfers between devices, shards(): down_full = lax.all_gather(down_weight, 'cand', axis=1, tiled=True)  34.9 us
  transfers between devices with their start and end apart: 9, of which 9 were waited for; matrix products, arithmetic and copies ran while one was open for 7% of the time, Pallas kernels for 0%

commit v1 on v0

--- a/solution.py
+++ b/solution.py
@@ -4,6 +4,18 @@
 from jax.sharding import PartitionSpec as P
 
 FF = 8192
+
+
+def ring_product(value, axis, dim, product):
+    size, index, extent = (lax.axis_size(axis), lax.axis_index(axis), value.shape[dim])
+    upward = [(i, (i + 1) % size) for i in range(size)]
+    current, so_far = (value, None)
+    for hop in range(size):
+        upcoming = lax.ppermute(current, axis, upward) if hop < size - 1 else None
+        update = product(current, (index - hop) % size * extent)
+        so_far = update if so_far is None else so_far + update
+        current = upcoming
+    return so_far
 
 
 def shards(tokens, cotangent, gate_weight, up_weight, down_weight, width_steps, block_order):
@@ -17,7 +29,6 @@
         lax.all_gather(gate_weight, "cand", axis=0, tiled=True),
         lax.all_gather(up_weight, "cand", axis=0, tiled=True),
     )
-    down_full = lax.all_gather(down_weight, "cand", axis=1, tiled=True)
     width = gate_weight.shape[1]
     places = jnp.arange(block_order.shape[0], dtype=jnp.int32)
     logical = jnp.sum(jnp.where(places == lax.axis_index("hid"), block_order, 0))
@@ -28,7 +39,17 @@
     sig = jax.nn.sigmoid(gate)
     act = keep * gate * sig
     hidden = (act * up).astype(jnp.bfloat16)
-    dhid = keep * jnp.einsum("td,fd->tf", upstream, down_full, preferred_element_type=jnp.float32)
+    dhid = keep * ring_product(
+        down_weight,
+        "cand",
+        1,
+        lambda own_block, start: jnp.einsum(
+            "td,fd->tf",
+            lax.dynamic_slice_in_dim(upstream, start, own_block.shape[1], axis=1),
+            own_block,
+            preferred_element_type=jnp.float32,
+        ),
+    )
     forward_d_up = (dhid * act).astype(jnp.bfloat16)
     forward_d_gate = (dhid * up * keep * sig * (1.0 + gate * (1.0 - sig))).astype(jnp.bfloat16)
     down_local = jnp.einsum("tf,td->fd", hidden, upstream, preferred_element_type=jnp.float32)

time: 423 us -> 389 us (0.920)
  waiting for transfers between devices: 367 us -> 330 us
    all_gather x1 -> x0, waiting for transfers between devices: 34.9 us -> none  [shards(): down_full = lax.all_gather(down_weight, 'cand', axis=1, tiled=True)]
    ppermute x0 -> x3, waiting for transfers between devices: none -> 14.6 us  [ring_product(): upcoming = lax.ppermute(current, axis, upward) if hop < size - 1 else None]
    all_gather x1, waiting for transfers between devices: 36.9 us -> 24.3 us  [shards(): lax.all_gather(cotangent, 'hid', axis=2, tiled=True)]
  transfers between devices with their start and end apart: 9 -> 11, of which waited for: 9 -> 9; matrix products, arithmetic and copies ran while one was open for 7% -> 8% of each run, Pallas kernels for 0% -> 0%
where the time goes in v1:
time: 389 us
  waiting for transfers between devices  330 us (85%)
  matrix products  28.9 us (7%)
  between operations  15.6 us (4%)
  local copies, waits for them, and re-layouts  7.6 us (2%)
  other arithmetic  5.75 us (1%)
    reduce_scatter x1, waiting for transfers between devices, shards(): lax.psum_scatter(input_part[None].astype(jnp.bfloat16), 'hid', scatter_di...  53.3 us
    reduce_scatter x1, waiting for transfers between devices, shards(): lax.psum_scatter(up_local.astype(jnp.bfloat16), 'cand', scatter_dimension...  44.4 us
    reduce_scatter x1, waiting for transfers between devices, shards(): lax.psum_scatter(down_local.astype(jnp.bfloat16), 'cand', scatter_dimensi...  44.4 us
    reduce_scatter x1, waiting for transfers between devices, shards(): lax.psum_scatter(gate_local.astype(jnp.bfloat16), 'cand', scatter_dimensi...  44.1 us
    all_gather x1, waiting for transfers between devices, shards(): lax.all_gather(tokens, 'hid', axis=2, tiled=True)  35.8 us
    all_gather x1, waiting for transfers between devices, shards(): lax.all_gather(gate_weight, 'cand', axis=0, tiled=True)  35.1 us
    all_gather x1, waiting for transfers between devices, shards(): lax.all_gather(up_weight, 'cand', axis=0, tiled=True)  31.2 us
    all_gather x1, waiting for transfers between devices, shards(): lax.all_gather(cotangent, 'hid', axis=2, tiled=True)  24.3 us
  transfers between devices with their start and end apart: 11, of which 9 were waited for; matrix products, arithmetic and copies ran while one was open for 8% of the time, Pallas kernels for 0%

profile of v1, /device:TPU:0, one launch (start us, length us, event | category | flops | bytes accessed | tf_op | source)
XLA Modules:
  0.0 388.6 jit_solution(6391795120514430836)
XLA Ops:
  7.2 0.0 all-gather.5.cloned.1.call-start
  7.2 0.7 all-gather.5.cloned.1.call-update
  7.9 0.0 all-gather.7.cloned.1.call-start
  7.9 0.7 all-gather.7.cloned.1.call-update
  8.6 0.0 all-gather.11.cloned.1.call-start
  8.7 0.7 all-gather.11.cloned.1.call-update
  9.4 0.0 all-gather.9.cloned.1.call-start
  9.4 0.5 all-gather.9.cloned.1.call-update
  10.0 0.0 reduce-scatter.5.cloned.1.call-start
  10.0 0.5 collective-permute-start
  10.6 14.6 %collective-permute-done = bf16[1024,512]{1,0:T(8,128)(2,1)S(1)} collective-permute-done((bf16[1024,512]{1,0:T(8,128)(2,1)}, bf16[1024,512]{1,0:T(8,128)(2,1)S(1)}, u32[]{:S(2)}, u32[]{:S(2)}) %collective-permute-start) | collective-permute-done | bytes 1048608 | tf_op jit(solution)/shard_map/ppermute | solution.py:14
  25.2 0.0 collective-permute-start.1
  25.9 1.3 fusion.23
  27.9 24.3 %all-gather.5.cloned.1.call-done = bf16[1,256,2048]{2,1,0:T(8,128)(2,1)} async-done(((bf16[1,256,256]{2,1,0:T(8,128)(2,1)}), bf16[1,256,2048]{2,1,0:T(8,128)(2,1)}) %all-gather.5.cloned.1.call-update) | async-done | bytes 1048592 | tf_op jit(solution)/shard_map/all_gather | solution.py:24
  52.2 1.8 fusion.13
  53.9 1.4 convolution_add_fusion.3
  55.4 0.1 collective-permute-start.2
  55.5 1.4 convolution_add_fusion.2
  56.9 35.8 %all-gather.7.cloned.1.call-done = bf16[1,256,2048]{2,1,0:T(8,128)(2,1)} async-done(((bf16[1,256,256]{2,1,0:T(8,128)(2,1)}), bf16[1,256,2048]{2,1,0:T(8,128)(2,1)}) %all-gather.7.cloned.1.call-update) | async-done | bytes 1048592 | tf_op jit(solution)/shard_map/all_gather | solution.py:23
  92.7 35.1 %all-gather.11.cloned.1.call-done = bf16[2048,1024]{1,0:T(8,128)(2,1)} async-done(((bf16[512,1024]{1,0:T(8,128)(2,1)}), bf16[2048,1024]{1,0:T(8,128)(2,1)}) %all-gather.11.cloned.1.call-update) | async-done | bytes 4194320 | tf_op jit(solution)/shard_map/all_gather | solution.py:29
  127.7 4.7 %fusion.6 = f32[256,1024]{1,0:T(8,128)} fusion(bf16[2048,1024]{1,0:T(8,128)(2,1)} %all-gather.11.cloned.1.call-done, bf16[1,256,2048]{2,1,0:T(8,128)(2,1)} %all-gather.7.cloned.1.call-done), kind=kOutput, calls=%fused_computation.13 | convolution fusion | flops 1073741824 | bytes 6291456 | tf_op jit(solution)/shard_map/dot_general | solution.py:37
  132.5 31.2 %all-gather.9.cloned.1.call-done = bf16[2048,1024]{1,0:T(8,128)(2,1)} async-done(((bf16[512,1024]{1,0:T(8,128)(2,1)}), bf16[2048,1024]{1,0:T(8,128)(2,1)}) %all-gather.9.cloned.1.call-update) | async-done | bytes 4194320 | tf_op jit(solution)/shard_map/all_gather | solution.py:30
  163.6 3.5 fusion.8
  167.2 2.6 multiply_convert_fusion.1
  169.8 0.3 copy-done.2
  170.1 1.3 fusion.25
  171.4 0.6 copy-done.3
  172.1 2.3 fusion.1
  174.3 0.0 reduce-scatter.5.cloned.1.call-update
  174.4 0.0 reduce-scatter.7.cloned.1.call-start
  174.4 3.2 convert_bitcast_fusion.1
  177.6 0.0 reduce-scatter.7.cloned.1.call-update
  177.7 0.0 reduce-scatter.9.cloned.1.call-start
  177.7 3.3 convert_bitcast_fusion
  181.0 0.0 reduce-scatter.9.cloned.1.call-update
  181.0 0.0 reduce-scatter.11.cloned.1.call-start
  181.1 1.2 copy-done.5
  182.3 0.3 copy-done.7
  182.6 3.3 convolution_convert_fusion
  185.9 0.0 reduce-scatter.11.cloned.1.call-update
  185.9 53.3 %reduce-scatter.5.cloned.1.call-done = bf16[1,256,256]{2,1,0:T(8,128)(2,1)} async-done(((bf16[1,256,2048]{2,1,0:T(8,128)(2,1)}), bf16[1,256,256]{2,1,0:T(8,128)(2,1)}) %reduce-scatter.5.cloned.1.call-update) | async-done | bytes 131088 | tf_op jit(solution)/shard_map/reduce_scatter | solution.py:64
  239.2 1.6 convert_element_type.50
  240.9 44.1 %reduce-scatter.7.cloned.1.call-done = bf16[512,1024]{0,1:T(8,128)(2,1)} async-done(((bf16[2048,1024]{0,1:T(8,128)(2,1)}), bf16[512,1024]{0,1:T(8,128)(2,1)}) %reduce-scatter.7.cloned.1.call-update) | async-done | bytes 1048592 | tf_op jit(solution)/shard_map/reduce_scatter | solution.py:68
  285.0 2.6 copy.11
  287.6 44.4 %reduce-scatter.9.cloned.1.call-done = bf16[512,1024]{0,1:T(8,128)(2,1)} async-done(((bf16[2048,1024]{0,1:T(8,128)(2,1)}), bf16[512,1024]{0,1:T(8,128)(2,1)}) %reduce-scatter.9.cloned.1.call-update) | async-done | bytes 1048592 | tf_op jit(solution)/shard_map/reduce_scatter | solution.py:71
  331.9 2.6 copy.12
  334.5 44.4 %reduce-scatter.11.cloned.1.call-done = bf16[1024,512]{1,0:T(8,128)(2,1)} async-done(((bf16[1024,2048]{1,0:T(8,128)(2,1)}), bf16[1024,512]{1,0:T(8,128)(2,1)}) %reduce-scatter.11.cloned.1.call-update) | async-done | bytes 1048592 | tf_op jit(solution)/shard_map/reduce_scatter | solution.py:75
  378.9 2.8 convert_element_type.59
  (14 shorter events, 0.0 us)
Async XLA Ops:
  7.2 45.0 %all-gather.5.cloned.1.call-start = ((), (), s32[]{:S(2)}) async-start(), calls=%async_computation.4 | async-start | bytes 1179648 | tf_op jit(solution)/shard_map/all_gather | solution.py:24
  7.9 84.8 %all-gather.7.cloned.1.call-start = ((), (), s32[]{:S(2)}) async-start(), calls=%async_computation.5 | async-start | bytes 1179648 | tf_op jit(solution)/shard_map/all_gather | solution.py:23
  8.6 119.1 %all-gather.11.cloned.1.call-start = ((), (), s32[]{:S(2)}) async-start(), calls=%async_computation.7 | async-start | bytes 5242880 | tf_op jit(solution)/shard_map/all_gather | solution.py:29
  9.4 154.3 %all-gather.9.cloned.1.call-start = ((), (), s32[]{:S(2)}) async-start(), calls=%async_computation.6 | async-start | bytes 5242880 | tf_op jit(solution)/shard_map/all_gather | solution.py:30
  10.0 229.3 %reduce-scatter.5.cloned.1.call-start = ((), (), s32[]{:S(2)}) async-start(), calls=%async_computation.8 | async-start | bytes 1179648 | tf_op jit(solution)/shard_map/reduce_scatter | solution.py:64
  10.0 15.2 %collective-permute-start = (bf16[1024,512]{1,0:T(8,128)(2,1)}, bf16[1024,512]{1,0:T(8,128)(2,1)S(1)}, u32[]{:S(2)}, u32[]{:S(2)}) collective-permute-start(bf16[1024,512]{1,0:T(8,128)(2,1)} %param.11), channel_id=1, source_target_pairs={{0,8},{8,16},{16,24},{24,0},{1,9},{9,17},{17,25},{25,1},{2,10},{10... | collective-permute-start | bytes 3145736 | tf_op jit(solution)/shard_map/ppermute | solution.py:14
  25.2 30.2 %collective-permute-start.1 = (bf16[1024,512]{1,0:T(8,128)(2,1)S(1)}, bf16[1024,512]{1,0:T(8,128)(2,1)S(1)}, u32[]{:S(2)}, u32[]{:S(2)}) collective-permute-start(bf16[1024,512]{1,0:T(8,128)(2,1)S(1)} %collective-permute-done), channel_id=1, source_target_pairs={{0,8},{8,16},{16,24},{24,0},{1,9},{9,17},{17,25},{25,1},{2,10},{10... | collective-permute-start | bytes 3145736 | tf_op jit(solution)/shard_map/ppermute | solution.py:14
  55.4 111.8 %collective-permute-start.2 = (bf16[1024,512]{1,0:T(8,128)(2,1)S(1)}, bf16[1024,512]{1,0:T(8,128)(2,1)}, u32[]{:S(2)}, u32[]{:S(2)}) collective-permute-start(bf16[1024,512]{1,0:T(8,128)(2,1)S(1)} %collective-permute-done.1), channel_id=1, source_target_pairs={{0,8},{8,16},{16,24},{24,0},{1,9},{9,17},{17,25},{25,1},{2,10},{10... | collective-permute-start | bytes 3145736 | tf_op jit(solution)/shard_map/ppermute | solution.py:14
  92.7 71.0 %copy-start = (bf16[1,256,2048]{2,1,0:T(8,128)(2,1)S(1)}, bf16[1,256,2048]{2,1,0:T(8,128)(2,1)}, u32[]{:S(2)}) copy-start(bf16[1,256,2048]{2,1,0:T(8,128)(2,1)} %all-gather.7.cloned.1.call-done) | copy-start | bytes 3145732
  163.6 3.6 copy-start.4
  167.2 2.6 copy-start.6
  167.2 3.0 copy-start.2
  169.8 2.3 copy-start.3
  174.4 110.6 %reduce-scatter.7.cloned.1.call-start = ((), (), s32[]{:S(2)}) async-start(), calls=%async_computation.9 | async-start | bytes 5242880 | tf_op jit(solution)/shard_map/reduce_scatter | solution.py:68
  177.7 3.4 copy-start.1
  177.7 154.3 %reduce-scatter.9.cloned.1.call-start = ((), (), s32[]{:S(2)}) async-start(), calls=%async_computation.10 | async-start | bytes 5242880 | tf_op jit(solution)/shard_map/reduce_scatter | solution.py:71
  181.0 1.2 copy-start.5
  181.0 1.6 copy-start.7
  181.0 197.9 %reduce-scatter.11.cloned.1.call-start = ((), (), s32[]{:S(2)}) async-start(), calls=%async_computation.11 | async-start | bytes 5242880 | tf_op jit(solution)/shard_map/reduce_scatter | solution.py:75
Sparse Core Ops, SparseCore 0:
  10.0 42.1 all-gather.4
  54.2 38.3 all-gather.6
  94.2 33.4 all-gather.10
  129.1 34.4 all-gather.8
  174.5 64.7 reduce-scatter.4
  241.6 43.3 reduce-scatter.6
  287.5 44.3 reduce-scatter.8
  334.5 44.3 reduce-scatter.10
